TPU v7x, 256 devices: a whole 4x4x8 slice. The times are simulated.
256 devices in a mesh: fsdp: 16 (over y, x), ctx: 16 (over z, core).
Axes of the slice: x: 4, y: 4, z: 8, core: 2. Of those that a mesh axis runs over, the one named last changes fastest.
Arguments:
- queries: bfloat16 [32768, 2048], P(('fsdp', 'ctx')), may hold values from -80 to 80
- keys: bfloat16 [32768, 2048], P(('fsdp', 'ctx')), may hold values from -4 to 4
- values: bfloat16 [32768, 2048], P(('fsdp', 'ctx')), may hold values from -6 to 6
- out_weight: bfloat16 [2048, 4096], P('fsdp'), may hold values from -0.125 to 0.125
- sessions: int32 [16, 2048], P('fsdp'), may hold values from 0 to 2, never falling along the last dimension, each value on 1 to 1536 neighbouring positions
Outputs:
- output: bfloat16 [32768, 4096], P(('fsdp', 'ctx'))
Inputs may be any that keep to these rules, and one draw needn't show every extreme that they name: Along each slab the session number never falls; each of the 3 sessions holds 1 to 1536 tokens and one holds exactly 1536.
All inputs are finite; a program needn't handle non-finite values.
Results may differ from a plain program's by a relative error of at most 0.007.
Values may be sent and summed in bfloat16 or wider, within the bound.
No kernel may reach another device: no remote copies, remote signals or barrier semaphores. Data moves between devices by JAX's collectives and lax.ppermute only.
A program may use at most 128 MiB of HBM per device.

v0:
```python
import math
import jax
import jax.numpy as jnp
from jax import lax
from jax.sharding import PartitionSpec as P

HDIM = 128


def per_device(queries, keys, values, out_weight, sessions):
    tokens_here = queries.shape[0]
    width = queries.shape[1]
    heads_here = width // HDIM
    scale = 1.0 / math.sqrt(HDIM)
    slab_ids = sessions[0]
    first_token = lax.axis_index("ctx") * tokens_here
    my_positions = first_token + jnp.arange(tokens_here, dtype=jnp.int32)
    my_ids = lax.dynamic_slice_in_dim(slab_ids, first_token, tokens_here)
    query_heads = jnp.transpose(queries.reshape(tokens_here, heads_here, HDIM), (1, 0, 2))
    start_state = (
        jnp.full((heads_here, tokens_here), -1e30, jnp.float32),
        jnp.zeros((heads_here, tokens_here), jnp.float32),
        jnp.zeros((heads_here, tokens_here, HDIM), jnp.float32),
    )
    key_piece = lax.all_gather(keys, "ctx", axis=0, tiled=True)
    value_piece = lax.all_gather(values, "ctx", axis=0, tiled=True)
    count = key_piece.shape[0]
    key_positions = jnp.arange(count, dtype=jnp.int32)
    allowed = (my_ids[:, None] == slab_ids[None, :]) & (
        key_positions[None, :] <= my_positions[:, None]
    )

    def update(current):
        key_heads = jnp.transpose(key_piece.reshape(count, heads_here, HDIM), (1, 0, 2))
        value_heads = jnp.transpose(value_piece.reshape(count, heads_here, HDIM), (1, 0, 2))

        def one_head(operands):
            query_head, key_head, value_head, row_max, row_total, accum = operands
            scores = jnp.dot(query_head, key_head.T, preferred_element_type=jnp.float32) * scale
            scores = jnp.where(allowed, scores, jnp.float32(-1e30))
            new_max = jnp.maximum(row_max, jnp.max(scores, axis=1))
            weights = jnp.where(allowed, jnp.exp(scores - new_max[:, None]), jnp.float32(0.0))
            factor = jnp.exp(row_max - new_max)
            new_total = row_total * factor + jnp.sum(weights, axis=1)
            added = jnp.dot(
                weights.astype(jnp.bfloat16), value_head, preferred_element_type=jnp.float32
            )
            return (new_max, new_total, accum * factor[:, None] + added)

        return lax.map(one_head, (query_heads, key_heads, value_heads) + tuple(current))

    row_max, row_total, accum = lax.cond(
        jnp.any(allowed), update, lambda current: current, start_state
    )
    finished = accum / row_total[:, :, None]
    attended = jnp.transpose(finished, (1, 0, 2)).reshape(tokens_here, width).astype(jnp.bfloat16)
    piece = lax.all_gather(out_weight, "fsdp", axis=0, tiled=True)
    projected = jnp.dot(attended, piece, preferred_element_type=jnp.float32)
    return projected.astype(jnp.bfloat16)


def solution(mesh):
    return jax.shard_map(
        per_device,
        mesh=mesh,
        in_specs=(
            P(("fsdp", "ctx"), None),
            P(("fsdp", "ctx"), None),
            P(("fsdp", "ctx"), None),
            P("fsdp", None),
            P("fsdp", None),
        ),
        out_specs=P(("fsdp", "ctx"), None),
        check_vma=False,
    )
```

profile of v0, /device:TPU:1, one launch (start us, length us, event | category | flops | bytes accessed | tf_op | source)
XLA Modules:
  0.0 274.5 jit_solution(3808026801106439446)
XLA Ops:
  6.5 2.0 copy.8
  8.7 2.0 copy.9
  12.1 1.7 fusion.16
  14.4 1.3 copy.10
  15.7 63.8 %all-gather.4.cloned.1.call-done = bf16[2048,2048]{0,1:T(8,128)(2,1)} async-done(((bf16[128,2048]{0,1:T(8,128)(2,1)}), bf16[2048,2048]{0,1:T(8,128)(2,1)}) %all-gather.4.cloned.1.call-update) | async-done | bytes 8388624 | tf_op jit(solution)/shard_map/all_gather | solution.py:25
  79.5 64.4 %all-gather.6.cloned.1.call-done = bf16[2048,2048]{0,1:T(8,128)(2,1)} async-done(((bf16[128,2048]{0,1:T(8,128)(2,1)}), bf16[2048,2048]{0,1:T(8,128)(2,1)}) %all-gather.6.cloned.1.call-update) | async-done | bytes 8388624 | tf_op jit(solution)/shard_map/all_gather | solution.py:26
  143.9 86.1 %conditional.1 = (f32[16,128]{1,0:T(8,128)}, f32[16,128,128]{1,2,0:T(8,128)}) conditional(s32[]{:T(128)} %convert_element_type.18, () %tuple.17, (bf16[2048,2048]{0,1:T(8,128)(2,1)}, bf16[2048,2048]{0,1:T(8,128)(2,1)}, bf16[16,128,128]{1,2,0:T(8,128)(2,1)S(1)}, pred[128,2048]{1,0:T(32,128)(4,1)S(1)}) %tuple.49), branch_computations={%region_1.0_spmd, %region_2.7_spmd} | conditional | flops 136593792 | bytes 5349073 | solution.py:52
  143.9 86.1 %while.11 = (s32[]{:T(128)}, f32[16,128]{1,0:T(8,128)}, f32[16,128,128]{1,2,0:T(8,128)}, bf16[16,128,128]{1,2,0:T(8,128)(2,1)S(1)}, bf16[16,2048,128]{1,2,0:T(8,...) while((s32[]{:T(128)}, f32[16,128]{1,0:T(8,128)}, ...), condition=%wide.region_6.6_spmd, body=%wide.region_3.5_spmd.sunk | while | flops 136593792 | bytes 5348977 | solution.py:50
  143.9 1.5 fusion.28
  147.1 1.4 fusion.30
  149.3 1.5 fusion.28
  152.5 1.4 fusion.30
  154.7 1.5 fusion.28
  157.9 1.4 fusion.30
  160.1 1.5 fusion.28
  163.3 1.5 fusion.30
  165.5 1.5 fusion.28
  168.7 1.5 fusion.30
  170.9 1.5 fusion.28
  174.1 1.5 fusion.30
  176.2 1.5 fusion.28
  179.4 1.4 fusion.30
  181.6 1.5 fusion.28
  184.8 1.4 fusion.30
  187.0 1.5 fusion.28
  188.9 1.3 dynamic_update_slice.12
  190.2 1.5 fusion.30
  192.4 1.5 fusion.28
  195.5 1.4 fusion.30
  197.7 1.5 fusion.28
  199.6 1.3 dynamic_update_slice.12
  200.9 1.4 fusion.30
  203.1 1.5 fusion.28
  205.0 1.3 dynamic_update_slice.12
  206.3 1.4 fusion.30
  208.5 1.5 fusion.28
  211.7 1.4 fusion.30
  213.9 1.5 fusion.28
  215.8 1.3 dynamic_update_slice.12
  217.1 1.4 fusion.30
  219.3 1.5 fusion.28
  221.2 1.3 dynamic_update_slice.12
  222.5 1.4 fusion.30
  224.7 1.5 fusion.28
  227.9 1.4 fusion.30
  230.0 1.3 divide_convert_fusion
  231.4 27.4 %all-gather.8.cloned.1.call-done = bf16[2048,4096]{1,0:T(8,128)(2,1)} async-done(((bf16[128,4096]{1,0:T(8,128)(2,1)}), bf16[2048,4096]{1,0:T(8,128)(2,1)}) %all-gather.8.cloned.1.call-update) | async-done | bytes 16777232 | tf_op jit(solution)/shard_map/all_gather | solution.py:57
  258.8 9.1 %convolution_convert_fusion = bf16[128,4096]{1,0:T(8,128)(2,1)} fusion(bf16[128,2048]{0,1:T(8,128)(2,1)S(1)} %bitcast.45, bf16[2048,4096]{1,0:T(8,128)(2,1)} %all-gather.8.cloned.1.call-done), kind=kOutput, calls=%fused_computation.22 | convolution fusion | flops 2148007936 | bytes 18350080 | tf_op jit(solution)/shard_map/dot_general | solution.py:58
  (101 shorter events, 33.9 us)
Async XLA Ops:
  6.5 73.0 %all-gather.4.cloned.1.call-start = ((), (), s32[]{:S(2)}) async-start(), calls=%async_computation | async-start | bytes 8912896 | tf_op jit(solution)/shard_map/all_gather | solution.py:25
  8.6 135.3 %all-gather.6.cloned.1.call-start = ((), (), s32[]{:S(2)}) async-start(), calls=%async_computation.1 | async-start | bytes 8912896 | tf_op jit(solution)/shard_map/all_gather | solution.py:26
  10.7 248.1 %all-gather.8.cloned.1.call-start = ((), (), s32[]{:S(2)}) async-start(), calls=%async_computation.2 | async-start | bytes 17825792 | tf_op jit(solution)/shard_map/all_gather | solution.py:57
Sparse Core Ops, SparseCore 0:
  9.1 70.3 all-gather.3
  81.2 62.6 all-gather.5
  146.4 112.4 all-gather.7
where the time goes:
time: 277 us; the launch traced here: 274 us
  waiting for transfers between devices  156 us (56%)
  matrix products  56 us (20%)
  local copies, waits for them, and re-layouts  38.5 us (14%)
  between operations  13.7 us (5%)
  other arithmetic  9.54 us (3%)
    all_gather x1, waiting for transfers between devices, per_device(): value_piece = lax.all_gather(values, 'ctx', axis=0, tiled=True)  64.4 us
    all_gather x1, waiting for transfers between devices, per_device(): key_piece = lax.all_gather(keys, 'ctx', axis=0, tiled=True)  63.8 us
    dynamic_update_slice x48, local copies, waits for them, and re-layouts, update(): lax.map(one_head, (query_heads, key_heads, value_heads) + tuple(current))  32.4 us
    all_gather x1, waiting for transfers between devices, per_device(): piece = lax.all_gather(out_weight, 'fsdp', axis=0, tiled=True)  27.4 us
    dot_general x16, matrix products, one_head(): jnp.dot(query_head, key_head.T, preferred_element_type=jnp.float32) * scale  23.7 us
    dot_general x16, matrix products, one_head(): jnp.dot(weights.astype(jnp.bfloat16), value_head, preferred_element_type=...  23.2 us
    dot_general x1, matrix products, per_device(): projected = jnp.dot(attended, piece, preferred_element_type=jnp.float32)  9.1 us
    reduce_sum x16, other arithmetic, one_head(): new_total = row_total * factor + jnp.sum(weights, axis=1)  6.21 us
  transfers between devices with their start and end apart: 3, of which 3 were waited for; matrix products, arithmetic and copies ran while one was open for 34% of the time, Pallas kernels for 0%

commit v1 on v0

--- a/solution.py
+++ b/solution.py
@@ -54,7 +54,8 @@
     )
     finished = accum / row_total[:, :, None]
     attended = jnp.transpose(finished, (1, 0, 2)).reshape(tokens_here, width).astype(jnp.bfloat16)
-    piece = lax.all_gather(out_weight, "fsdp", axis=0, tiled=True)
+    h_now = jnp.stack([out_weight for _ in range(lax.psum(1, "fsdp"))], axis=0)
+    piece = jnp.concatenate(lax.all_to_all(h_now, "fsdp", 0, 0), axis=0)
     projected = jnp.dot(attended, piece, preferred_element_type=jnp.float32)
     return projected.astype(jnp.bfloat16)
 

time: 277 us -> 293 us (1.058)
  matrix products: 56 us -> 66.3 us
  starting transfers between devices: 0.09 us -> 7.81 us
  local copies, waits for them, and re-layouts: 38.5 us -> 31.5 us
  waiting for transfers between devices: 156 us -> 163 us
    all_to_all x0 -> x1, waiting for transfers between devices: none -> 47.5 us  [per_device(): piece = jnp.concatenate(lax.all_to_all(h_now, 'fsdp', 0, 0), axis=0)]
    all_gather x1 -> x0, waiting for transfers between devices: 27.4 us -> none  [per_device(): piece = lax.all_gather(out_weight, 'fsdp', axis=0, tiled=True)]
    all_gather x1, waiting for transfers between devices: 63.8 us -> 51.1 us  [per_device(): key_piece = lax.all_gather(keys, 'ctx', axis=0, tiled=True)]
    dynamic_update_slice x48 -> x16, local copies, waits for them, and re-layouts: 32.4 us -> 20.3 us  [update(): lax.map(one_head, (query_heads, key_heads, value_heads) + tuple(current))]
    dot_general x16, matrix products: 23.2 us -> 33.3 us  [one_head(): jnp.dot(weights.astype(jnp.bfloat16), value_head, preferred_element_type=...]
    all_to_all x0 -> x1, starting transfers between devices: none -> 7.77 us  [per_device(): piece = jnp.concatenate(lax.all_to_all(h_now, 'fsdp', 0, 0), axis=0)]
    another operation x0 -> x1, local copies, waits for them, and re-layouts: none -> 6.81 us  [per_device(): h_now = jnp.stack([out_weight for _ in range(lax.psum(1, 'fsdp'))], axis=0)]
  transfers between devices with their start and end apart: 3 -> 3, of which waited for: 3 -> 3; matrix products, arithmetic and copies ran while one was open for 34% -> 32% of each run, Pallas kernels for 0% -> 0%
where the time goes in v1:
time: 293 us; the launch traced here: 290 us
  waiting for transfers between devices  163 us (56%)
  matrix products  66.3 us (23%)
  local copies, waits for them, and re-layouts  31.5 us (11%)
  between operations  14.1 us (5%)
  starting transfers between devices  7.81 us (3%)
  other arithmetic  7.57 us (3%)
    all_gather x1, waiting for transfers between devices, per_device(): value_piece = lax.all_gather(values, 'ctx', axis=0, tiled=True)  64.3 us
    all_gather x1, waiting for transfers between devices, per_device(): key_piece = lax.all_gather(keys, 'ctx', axis=0, tiled=True)  51.1 us
    all_to_all x1, waiting for transfers between devices, per_device(): piece = jnp.concatenate(lax.all_to_all(h_now, 'fsdp', 0, 0), axis=0)  47.5 us
    dot_general x16, matrix products, one_head(): jnp.dot(weights.astype(jnp.bfloat16), value_head, preferred_element_type=...  33.3 us
    dot_general x16, matrix products, one_head(): jnp.dot(query_head, key_head.T, preferred_element_type=jnp.float32) * scale  23.6 us
    dynamic_update_slice x16, local copies, waits for them, and re-layouts, update(): lax.map(one_head, (query_heads, key_heads, value_heads) + tuple(current))  20.3 us
    dot_general x1, matrix products, per_device(): projected = jnp.dot(attended, piece, preferred_element_type=jnp.float32)  9.49 us
    all_to_all x1, starting transfers between devices, per_device(): piece = jnp.concatenate(lax.all_to_all(h_now, 'fsdp', 0, 0), axis=0)  7.77 us
  transfers between devices with their start and end apart: 3, of which 3 were waited for; matrix products, arithmetic and copies ran while one was open for 32% of the time, Pallas kernels for 0%

profile of v1, /device:TPU:1, one launch (start us, length us, event | category | flops | bytes accessed | tf_op | source)
XLA Modules:
  0.0 290.5 jit_solution(2970328275958009456)
XLA Ops:
  6.5 2.0 copy.8
  8.7 2.0 copy.9
  10.7 6.8 %stack.2 = bf16[16,128,4096]{2,1,0:T(8,128)(2,1)} broadcast(bf16[128,4096]{1,0:T(8,128)(2,1)} %param.12), dimensions={1,2} | broadcast | bytes 17825792 | tf_op jit(solution)/shard_map/stack | solution.py:57
  17.5 7.8 %all-to-all-start = ((bf16[16,128,4096]{2,1,0:T(8,128)(2,1)}), bf16[16,128,4096]{2,1,0:T(8,128)(2,1)}, u32[]{:S(2)}, u32[]{:S(2)}) async-start(bf16[16,128,4096]{2,1,0:T(8,128)(2,1)} %stack.2), calls=%async_computation | async-start | bytes 33554432 | tf_op jit(solution)/shard_map/all_to_all | solution.py:58
  27.4 51.1 %all-gather.3.cloned.1.call-done = bf16[2048,2048]{0,1:T(8,128)(2,1)} async-done(((bf16[128,2048]{0,1:T(8,128)(2,1)}), bf16[2048,2048]{0,1:T(8,128)(2,1)}) %all-gather.3.cloned.1.call-update) | async-done | bytes 8388624 | tf_op jit(solution)/shard_map/all_gather | solution.py:25
  78.5 64.3 %all-gather.5.cloned.1.call-done = bf16[2048,2048]{0,1:T(8,128)(2,1)} async-done(((bf16[128,2048]{0,1:T(8,128)(2,1)}), bf16[2048,2048]{0,1:T(8,128)(2,1)}) %all-gather.5.cloned.1.call-update) | async-done | bytes 8388624 | tf_op jit(solution)/shard_map/all_gather | solution.py:26
  142.8 83.8 %conditional.1 = (f32[16,128]{1,0:T(8,128)}, f32[16,128,128]{2,1,0:T(8,128)}) conditional(s32[]{:T(128)} %convert_element_type.16, () %tuple.17, (bf16[2048,2048]{0,1:T(8,128)(2,1)}, bf16[2048,2048]{0,1:T(8,128)(2,1)}, bf16[16,128,128]{1,2,0:T(8,128)(2,1)S(1)}, pred[128,2048]{1,0:T(32,128)(4,1)S(1)}) %tuple.45), branch_computations={%region_1.0_spmd, %region_2.7_spmd} | conditional | flops 136593792 | bytes 5087945 | solution.py:52
  142.8 83.8 %while.11 = (s32[]{:T(128)}, f32[16,128]{1,0:T(8,128)}, f32[16,128,128]{2,1,0:T(8,128)}, bf16[16,128,128]{1,2,0:T(8,128)(2,1)S(1)}, bf16[16,2048,128]{1,2,0:T(8,...) while((s32[]{:T(128)}, f32[16,128]{1,0:T(8,128)}, ...), condition=%wide.region_6.6_spmd, body=%wide.region_3.5_spmd.sunk | while | flops 136593792 | bytes 5087849 | solution.py:50
  142.8 1.5 fusion.30
  144.7 2.1 fusion.32
  148.1 1.5 fusion.30
  149.9 2.1 fusion.32
  153.3 1.5 fusion.30
  155.2 2.1 fusion.32
  158.5 1.5 fusion.30
  160.4 2.1 fusion.32
  163.8 1.5 fusion.30
  165.6 2.1 fusion.32
  169.0 1.5 fusion.30
  170.9 2.1 fusion.32
  174.2 1.5 fusion.30
  176.1 2.1 fusion.32
  179.4 1.5 fusion.30
  181.3 2.1 fusion.32
  184.7 1.5 fusion.30
  186.5 2.1 fusion.32
  188.6 1.3 dynamic_update_slice.12
  189.9 1.5 fusion.30
  191.8 2.1 fusion.32
  193.9 1.3 dynamic_update_slice.12
  195.1 1.5 fusion.30
  197.0 2.1 fusion.32
  199.1 1.3 dynamic_update_slice.12
  200.4 1.5 fusion.30
  202.3 2.1 fusion.32
  204.3 1.3 dynamic_update_slice.12
  205.6 1.5 fusion.30
  207.5 2.1 fusion.32
  209.6 1.3 dynamic_update_slice.12
  210.9 1.5 fusion.30
  212.7 2.1 fusion.32
  216.1 1.5 fusion.30
  218.0 2.1 fusion.32
  221.4 1.5 fusion.30
  223.2 2.1 fusion.32
  225.3 1.3 dynamic_update_slice.12
  226.6 47.5 %all-to-all-done = bf16[16,128,4096]{2,1,0:T(8,128)(2,1)} async-done(((bf16[16,128,4096]{2,1,0:T(8,128)(2,1)}), bf16[16,128,4096]{2,1,0:T(8,128)(2,1)}, u32[]{:S(2)}, u32[]{:S(2)}) %all-to-all-start) | async-done | bytes 16777248 | tf_op jit(solution)/shard_map/all_to_all | solution.py:58
  274.2 9.5 %fusion.17 = bf16[128,4096]{1,0:T(8,128)(2,1)} fusion(bf16[16,128,4096]{2,1,0:T(8,128)(2,1)} %all-to-all-done, f32[16,128,128]{2,1,0:T(8,128)} %get-tuple-element.57, f32[16,128]{1,0:T(8,128)} %get-tuple-element.58), kind=kOutput, calls=%fused_computation.23 | convolution fusion | flops 2148532224 | bytes 18882560 | tf_op jit(solution)/shard_map/dot_general | solution.py:59
  (72 shorter events, 20.6 us)
Async XLA Ops:
  6.5 72.0 %all-gather.3.cloned.1.call-start = ((), (), s32[]{:S(2)}) async-start(), calls=%async_computation.1 | async-start | bytes 8912896 | tf_op jit(solution)/shard_map/all_gather | solution.py:25
  8.6 134.2 %all-gather.5.cloned.1.call-start = ((), (), s32[]{:S(2)}) async-start(), calls=%async_computation.2 | async-start | bytes 8912896 | tf_op jit(solution)/shard_map/all_gather | solution.py:26
  17.5 7.8 %copy-start.1 = (s32[1,2048]{1,0:T(1,128)S(1)}, s32[1,2048]{1,0:T(1,128)}, u32[]{:S(2)}) copy-start(s32[1,2048]{1,0:T(1,128)} %param.13) | copy-start | bytes 24580
  17.5 9.6 %copy-start = (bf16[128,2048]{1,0:T(8,128)(2,1)S(1)}, bf16[128,2048]{1,0:T(8,128)(2,1)}, u32[]{:S(2)}) copy-start(bf16[128,2048]{1,0:T(8,128)(2,1)} %param.9) | copy-start | bytes 1572868
  17.5 256.6 %all-to-all-start = ((bf16[16,128,4096]{2,1,0:T(8,128)(2,1)}), bf16[16,128,4096]{2,1,0:T(8,128)(2,1)}, u32[]{:S(2)}, u32[]{:S(2)}) async-start(bf16[16,128,4096]{2,1,0:T(8,128)(2,1)} %stack.2), calls=%async_computation | async-start | bytes 33554432 | tf_op jit(solution)/shard_map/all_to_all | solution.py:58
Sparse Core Ops, SparseCore 0:
  9.1 69.3 all-gather.2
  80.3 62.5 all-gather.4
